TPU v7x, 32 devices: a whole 2x2x4 slice. The times are simulated.
32 devices in a mesh: dp: 8 (over z, x), table: 4 (over y, core).
Axes of the slice: x: 2, y: 2, z: 4, core: 2. Of those that a mesh axis runs over, the one named last changes fastest.
Arguments:
- feature_high: int32 [20, 2048], P(None, 'dp'), may hold values from 0 to 2047
- feature_low: int32 [20, 2048], P(None, 'dp'), may hold values from 0 to 2047
- labels: int32 [2048], P('dp'), may hold values 0 or 1
- weights: float32 [4194304], P(('dp', 'table')), may hold values from -0.6 to 0.6
- history_steps: float32 [8, 4194304], P(None, ('dp', 'table')), may hold values from -46 to 46
- history_diffs: float32 [8, 4194304], P(None, ('dp', 'table')), may hold values from -198 to 198, as said below
Outputs:
- direction: float32 [4194304], P(('dp', 'table'))
Inputs may be any that keep to these rules, and one draw needn't show every extreme that they name: Each entry of history_diffs has the sign of the matching entry of history_steps and 0.2 to 4.3 times its magnitude.
All inputs are finite; a program needn't handle non-finite values. No bound on the sum of `labels` on one device may be relied on, other than what follows from the above.
Results may differ from a plain program's by a relative error of at most 0.0001.
Values sent between devices are 32-bit elements; how exact they have to be, the bound alone decides.
A program may use at most 64 MiB of HBM per device.

v0:
```python
import jax
import jax.numpy as jnp
from jax import lax
from jax.sharding import PartitionSpec as P

TABLE = 4194304
HASHES = 4
high_mult = (40503, 96469, 255361, 362443)
low_mult = (2053, 6151, 12289, 98317)
slot_mult = (1543, 3079, 769, 3457)
shifts = (0, 1048573, 2097143, 3145727)
l2_weight = 1.0


def hashed(feature_high, feature_low, number):
    slot_index = jnp.arange(feature_high.shape[0], dtype=jnp.int32)[:, None]
    part_high = feature_high * high_mult[number] % TABLE
    part_low = feature_low * low_mult[number] % TABLE
    return (part_high + part_low + slot_index * slot_mult[number] + shifts[number]) % TABLE


def local(feature_high, feature_low, labels, weights, history_steps, history_diffs):
    width = weights.shape[0]
    shard_count = lax.axis_size("table")
    column = lax.axis_index("table")
    gathered = lax.all_gather(weights, "dp", axis=0, tiled=True)
    margin = jnp.zeros((feature_high.shape[1],), jnp.float32)
    owned_list = []
    position_list = []
    for number in range(HASHES):
        indices = hashed(feature_high, feature_low, number)
        blocks = indices // width
        owned = blocks % shard_count == column
        position = blocks // shard_count * width + indices % width
        owned_list.append(owned)
        position_list.append(position)
        margin = margin + jnp.sum(jnp.where(owned, gathered[position], 0.0), axis=0)
    margin = lax.psum(margin, "table")
    residual = jax.nn.sigmoid(margin) - labels.astype(jnp.float32)
    all_positions = jnp.concatenate([place.reshape(-1) for place in position_list])
    all_terms = jnp.concatenate(
        [jnp.where(owned, residual[None, :], 0.0).reshape(-1) for owned in owned_list]
    )
    partial_grad = jnp.zeros(gathered.shape, jnp.float32).at[all_positions].add(all_terms)
    summed = lax.psum(partial_grad, "dp")
    mine = lax.dynamic_slice_in_dim(summed, lax.axis_index("dp") * width, width)
    gradient = mine + l2_weight * weights
    memory = history_steps.shape[0]
    newest = memory - 1
    pair_sums, newest_square = lax.psum(
        (
            jnp.sum(history_steps * history_diffs, axis=1),
            jnp.sum(history_diffs[newest] * history_diffs[newest]),
        ),
        ("dp", "table"),
    )
    inverse = 1.0 / pair_sums
    current = gradient
    alphas = [None] * memory
    for which in reversed(range(memory)):
        alphas[which] = inverse[which] * lax.psum(
            jnp.sum(history_steps[which] * current), ("dp", "table")
        )
        current = current - alphas[which] * history_diffs[which]
    current = pair_sums[newest] / newest_square * current
    for which in range(memory):
        correction = inverse[which] * lax.psum(
            jnp.sum(history_diffs[which] * current), ("dp", "table")
        )
        current = current + (alphas[which] - correction) * history_steps[which]
    return -current


def solution(mesh):
    placed = (
        P(None, "dp"),
        P(None, "dp"),
        P("dp"),
        P(("dp", "table")),
        P(None, ("dp", "table")),
        P(None, ("dp", "table")),
    )
    return jax.shard_map(
        local, mesh=mesh, in_specs=placed, out_specs=P(("dp", "table")), check_vma=False
    )
```

profile of v0, /device:TPU:0, one launch (start us, length us, event | category | flops | bytes accessed | tf_op | source)
XLA Modules:
  0.0 1326.4 jit_solution(4070910795745092147)
XLA Ops:
  8.8 76.8 %all-gather.2.cloned.1.call-done = f32[1048576]{0:T(1024)} async-done(((f32[131072]{0:T(1024)}), f32[1048576]{0:T(1024)}) %all-gather.2.cloned.1.call-update) | async-done | bytes 4194320 | tf_op jit(solution)/shard_map/all_gather | solution.py:26
  85.6 60.4 %gather_fusion.3 = f32[5120]{0:T(1024)S(1)} fusion(f32[1048576]{0:T(1024)} %all-gather.2.cloned.1.call-done, s32[5120]{0:T(1024)S(1)} %broadcast_clamp_fusion), kind=kCustom, calls=%fused_computation.3 | custom fusion | bytes 61440 | tf_op jit(solution)/shard_map/gather | solution.py:37
  146.0 60.4 %gather_fusion.1 = f32[5120]{0:T(1024)S(1)} fusion(f32[1048576]{0:T(1024)} %all-gather.2.cloned.1.call-done, s32[5120]{0:T(1024)S(1)} %broadcast_clamp_fusion.2), kind=kCustom, calls=%fused_computation.1 | custom fusion | bytes 61440 | tf_op jit(solution)/shard_map/gather | solution.py:37
  206.5 60.4 %gather_fusion = f32[5120]{0:T(1024)S(1)} fusion(f32[1048576]{0:T(1024)} %all-gather.2.cloned.1.call-done, s32[5120]{0:T(1024)S(1)} %broadcast_clamp_fusion.3), kind=kCustom, calls=%fused_computation | custom fusion | bytes 61440 | tf_op jit(solution)/shard_map/gather | solution.py:37
  266.9 60.4 %gather_fusion.2 = f32[5120]{0:T(1024)S(1)} fusion(f32[1048576]{0:T(1024)} %all-gather.2.cloned.1.call-done, s32[5120]{0:T(1024)S(1)} %broadcast_clamp_fusion.1), kind=kCustom, calls=%fused_computation.2 | custom fusion | bytes 61440 | tf_op jit(solution)/shard_map/gather | solution.py:37
  333.3 109.3 %scatter_custom_fusion = f32[1048576]{0:T(1024)} fusion(s32[20480]{0:T(1024)S(1)} %bitcast.84, f32[20480]{0:T(1024)S(1)} %pad_maximum_fusion, f32[]{:T(128)} %constant.207.clone.1), kind=kCustom, calls=%fused_computation.6 | custom fusion | flops 20480 | bytes 4194308 | tf_op jit(solution)/shard_map/scatter-add | solution.py:44
  463.9 133.7 %all-reduce.4.cloned.1.call-done = f32[1048576]{0:T(1024)} async-done(((f32[1048576]{0:T(1024)}), f32[1048576]{0:T(1024)}) %all-reduce.4.cloned.1.call-update) | async-done | bytes 4194320 | tf_op jit(solution)/shard_map/psum | solution.py:45
  599.4 16.6 %fusion.61 = (f32[1,131072]{1,0:T(1,128)}, f32[1,131072]{1,0:T(1,128)S(1)}, f32[1,131072]{1,0:T(1,128)}, f32[1,131072]{1,0:T(1,128)S(1)}, f32[1,131072]{1,0:T(1,...) fusion(f32[8,131072]{1,0:T(8,128)} %param.11), kind=kLoop, calls=%fused_computation.206 | loop fusion | bytes 8388608 | tf_op jit(solution)/shard_map/slice | solution.py:64
  616.0 39.4 %all-reduce.1 = (f32[8]{0:T(128)S(1)}, f32[]{:T(128)}) all-reduce(f32[8]{0:T(128)S(1)} %multiply_reduce_fusion, f32[]{:T(128)} %multiply_reduce_fusion.16), channel_id=1, replica_groups=mesh['dp'=8,'table'=4] {'dp','table'}, use_global_device_ids=true, to_apply=%region_1.2 | all-reduce | flops 9 | bytes 72 | tf_op jit(solution)/shard_map/psum | solution.py:50
  660.4 40.3 %psum.145 = f32[]{:T(128)} all-reduce(f32[]{:T(128)} %get-tuple-element.23), channel_id=1, replica_groups=mesh['dp'=8,'table'=4] {'dp','table'}, use_global_device_ids=true, to_apply=%region_14.15 | all-reduce | flops 1 | bytes 8 | tf_op jit(solution)/shard_map/psum | solution.py:61
  703.8 40.7 %psum.146 = f32[]{:T(128)} all-reduce(f32[]{:T(128)} %multiply_reduce_fusion.14), channel_id=1, replica_groups=mesh['dp'=8,'table'=4] {'dp','table'}, use_global_device_ids=true, to_apply=%region_16.17 | all-reduce | flops 1 | bytes 8 | tf_op jit(solution)/shard_map/psum | solution.py:61
  748.7 40.4 %psum.147 = f32[]{:T(128)} all-reduce(f32[]{:T(128)} %get-tuple-element.21), channel_id=1, replica_groups=mesh['dp'=8,'table'=4] {'dp','table'}, use_global_device_ids=true, to_apply=%region_18.19 | all-reduce | flops 1 | bytes 8 | tf_op jit(solution)/shard_map/psum | solution.py:61
  792.3 40.6 %psum.148 = f32[]{:T(128)} all-reduce(f32[]{:T(128)} %multiply_reduce_fusion.12), channel_id=1, replica_groups=mesh['dp'=8,'table'=4] {'dp','table'}, use_global_device_ids=true, to_apply=%region_20.21 | all-reduce | flops 1 | bytes 8 | tf_op jit(solution)/shard_map/psum | solution.py:61
  837.1 40.3 %psum.149 = f32[]{:T(128)} all-reduce(f32[]{:T(128)} %get-tuple-element.19), channel_id=1, replica_groups=mesh['dp'=8,'table'=4] {'dp','table'}, use_global_device_ids=true, to_apply=%region_22.23 | all-reduce | flops 1 | bytes 8 | tf_op jit(solution)/shard_map/psum | solution.py:61
  881.2 40.6 %psum.150 = f32[]{:T(128)} all-reduce(f32[]{:T(128)} %multiply_reduce_fusion.10), channel_id=1, replica_groups=mesh['dp'=8,'table'=4] {'dp','table'}, use_global_device_ids=true, to_apply=%region_24.25 | all-reduce | flops 1 | bytes 8 | tf_op jit(solution)/shard_map/psum | solution.py:61
  926.0 40.2 %all-reduce = (f32[]{:T(128)}, f32[]{:T(128)}) all-reduce(f32[]{:T(128)} %get-tuple-element.17, f32[]{:T(128)} %get-tuple-element.61), channel_id=1, replica_groups=mesh['dp'=8,'table'=4] {'dp','table'}, use_global_device_ids=true, to_apply=%region_26.27 | all-reduce | flops 2 | bytes 16 | tf_op jit(solution)/shard_map/psum | solution.py:61
  970.7 40.6 %psum.152 = f32[]{:T(128)} all-reduce(f32[]{:T(128)} %multiply_reduce_fusion.8), channel_id=1, replica_groups=mesh['dp'=8,'table'=4] {'dp','table'}, use_global_device_ids=true, to_apply=%region_28.29 | all-reduce | flops 1 | bytes 8 | tf_op jit(solution)/shard_map/psum | solution.py:67
  1015.6 40.1 %psum.153 = f32[]{:T(128)} all-reduce(f32[]{:T(128)} %get-tuple-element.15), channel_id=1, replica_groups=mesh['dp'=8,'table'=4] {'dp','table'}, use_global_device_ids=true, to_apply=%region_30.31 | all-reduce | flops 1 | bytes 8 | tf_op jit(solution)/shard_map/psum | solution.py:67
  1058.8 40.7 %psum.154 = f32[]{:T(128)} all-reduce(f32[]{:T(128)} %multiply_reduce_fusion.6), channel_id=1, replica_groups=mesh['dp'=8,'table'=4] {'dp','table'}, use_global_device_ids=true, to_apply=%region_32.33 | all-reduce | flops 1 | bytes 8 | tf_op jit(solution)/shard_map/psum | solution.py:67
  1103.7 40.1 %psum.155 = f32[]{:T(128)} all-reduce(f32[]{:T(128)} %get-tuple-element.13), channel_id=1, replica_groups=mesh['dp'=8,'table'=4] {'dp','table'}, use_global_device_ids=true, to_apply=%region_34.35 | all-reduce | flops 1 | bytes 8 | tf_op jit(solution)/shard_map/psum | solution.py:67
  1147.2 40.7 %psum.156 = f32[]{:T(128)} all-reduce(f32[]{:T(128)} %multiply_reduce_fusion.4), channel_id=1, replica_groups=mesh['dp'=8,'table'=4] {'dp','table'}, use_global_device_ids=true, to_apply=%region_36.37 | all-reduce | flops 1 | bytes 8 | tf_op jit(solution)/shard_map/psum | solution.py:67
  1191.4 40.2 %psum.157 = f32[]{:T(128)} all-reduce(f32[]{:T(128)} %get-tuple-element.11), channel_id=1, replica_groups=mesh['dp'=8,'table'=4] {'dp','table'}, use_global_device_ids=true, to_apply=%region_38.39 | all-reduce | flops 1 | bytes 8 | tf_op jit(solution)/shard_map/psum | solution.py:67
  1233.7 40.6 %psum.158 = f32[]{:T(128)} all-reduce(f32[]{:T(128)} %multiply_reduce_fusion.2), channel_id=1, replica_groups=mesh['dp'=8,'table'=4] {'dp','table'}, use_global_device_ids=true, to_apply=%region_40.41 | all-reduce | flops 1 | bytes 8 | tf_op jit(solution)/shard_map/psum | solution.py:67
  1277.3 40.1 %psum.159 = f32[]{:T(128)} all-reduce(f32[]{:T(128)} %get-tuple-element.9), channel_id=1, replica_groups=mesh['dp'=8,'table'=4] {'dp','table'}, use_global_device_ids=true, to_apply=%region_42.43 | all-reduce | flops 1 | bytes 8 | tf_op jit(solution)/shard_map/psum | solution.py:67
  (73 shorter events, 67.1 us)
Async XLA Ops:
  6.5 79.1 %all-gather.2.cloned.1.call-start = ((), (), s32[]{:S(2)}) async-start(), calls=%async_computation | async-start | bytes 4718592 | tf_op jit(solution)/shard_map/all_gather | solution.py:26
  7.3 590.4 %all-reduce.4.cloned.1.call-start = ((), (), s32[]{:S(2)}) async-start(), calls=%async_computation.1 | async-start | bytes 8388608 | tf_op jit(solution)/shard_map/psum | solution.py:45
  266.9 66.3 %copy-start.4 = (s32[256]{0:T(256)S(1)}, s32[256]{0:T(256)}, u32[]{:S(2)}) copy-start(s32[256]{0:T(256)} %param.8) | copy-start | bytes 3076
  459.1 138.6 %copy-start = (f32[1,131072]{1,0:T(1,128)}, f32[1,131072]{1,0:T(1,128)S(1)}, u32[]{:S(2)}) copy-start(f32[1,131072]{1,0:T(1,128)S(1)} %get-tuple-element.59) | copy-start | bytes 1572868
  459.1 138.6 %copy-start.3 = (f32[131072]{0:T(1024)S(1)}, f32[131072]{0:T(1024)}, u32[]{:S(2)}) copy-start(f32[131072]{0:T(1024)} %param.9) | copy-start | bytes 1572868
  1100.8 174.7 %copy-start.2 = (f32[1,131072]{1,0:T(1,128)S(1)}, f32[1,131072]{1,0:T(1,128)}, u32[]{:S(2)}) copy-start(f32[1,131072]{1,0:T(1,128)} %get-tuple-element.58) | copy-start | bytes 1572868
  1145.3 173.4 %copy-start.1 = (f32[1,131072]{1,0:T(1,128)S(1)}, f32[1,131072]{1,0:T(1,128)}, u32[]{:S(2)}) copy-start(f32[1,131072]{1,0:T(1,128)} %copy-done) | copy-start | bytes 1572868
Sparse Core Ops, SparseCore 0:
  9.5 76.0 all-gather.1
  442.8 154.8 all-reduce.3
where the time goes:
time: 1340 us; the launch traced here: 1330 us
  blocking collectives  651 us (49%)
  local copies, waits for them, and re-layouts  276 us (21%)
  waiting for transfers between devices  211 us (16%)
  other arithmetic  152 us (11%)
  between operations  35.7 us (3%)
    psum x8, blocking collectives, local(): lax.psum(jnp.sum(history_diffs[which] * current), ('dp', 'table'))  323 us
    psum x7, blocking collectives, local(): lax.psum(jnp.sum(history_steps[which] * current), ('dp', 'table'))  283 us
    gather x8, local copies, waits for them, and re-layouts, local(): margin = margin + jnp.sum(jnp.where(owned, gathered[position], 0.0), axis=0)  242 us
    psum x1, waiting for transfers between devices, local(): summed = lax.psum(partial_grad, 'dp')  134 us
    scatter-add x1, other arithmetic, local(): jnp.zeros(gathered.shape, jnp.float32).at[all_positions].add(all_terms)  109 us
    all_gather x1, waiting for transfers between devices, local(): gathered = lax.all_gather(weights, 'dp', axis=0, tiled=True)  76.8 us
    psum x1, blocking collectives, local(): lax.psum((jnp.sum(history_steps * history_diffs, axis=1), jnp.sum(history...  39.4 us
  transfers between devices with their start and end apart: 2, of which 2 were waited for; matrix products, arithmetic and copies ran while one was open for 2% of the time, Pallas kernels for 0%

commit v1 on v0

--- a/solution.py
+++ b/solution.py
@@ -23,7 +23,9 @@
     width = weights.shape[0]
     shard_count = lax.axis_size("table")
     column = lax.axis_index("table")
-    gathered = lax.all_gather(weights, "dp", axis=0, tiled=True)
+    gathered = jnp.concatenate(
+        lax.all_to_all(jnp.stack([weights] * lax.axis_size("dp")), "dp", 0, 0), axis=0
+    )
     margin = jnp.zeros((feature_high.shape[1],), jnp.float32)
     owned_list = []
     position_list = []

time: 1340 us -> 1360 us (1.015)
  waiting for transfers between devices: 211 us -> 227 us
    all_to_all x0 -> x1, waiting for transfers between devices: none -> 92.5 us  [local(): lax.all_to_all(jnp.stack([weights] * lax.axis_size('dp')), 'dp', 0, 0)]
    all_gather x1 -> x0, waiting for transfers between devices: 76.8 us -> none  [local(): gathered = lax.all_gather(weights, 'dp', axis=0, tiled=True)]
where the time goes in v1:
time: 1360 us; the launch traced here: 1350 us
  blocking collectives  651 us (48%)
  local copies, waits for them, and re-layouts  281 us (21%)
  waiting for transfers between devices  227 us (17%)
  other arithmetic  151 us (11%)
  between operations  35.7 us (3%)
    psum x8, blocking collectives, local(): lax.psum(jnp.sum(history_diffs[which] * current), ('dp', 'table'))  323 us
    psum x7, blocking collectives, local(): lax.psum(jnp.sum(history_steps[which] * current), ('dp', 'table'))  283 us
    gather x8, local copies, waits for them, and re-layouts, local(): margin = margin + jnp.sum(jnp.where(owned, gathered[position], 0.0), axis=0)  242 us
    psum x1, waiting for transfers between devices, local(): summed = lax.psum(partial_grad, 'dp')  134 us
    scatter-add x1, other arithmetic, local(): jnp.zeros(gathered.shape, jnp.float32).at[all_positions].add(all_terms)  109 us
    all_to_all x1, waiting for transfers between devices, local(): lax.all_to_all(jnp.stack([weights] * lax.axis_size('dp')), 'dp', 0, 0)  92.5 us
    psum x1, blocking collectives, local(): lax.psum((jnp.sum(history_steps * history_diffs, axis=1), jnp.sum(history...  39.4 us
  transfers between devices with their start and end apart: 2, of which 2 were waited for; matrix products, arithmetic and copies ran while one was open for 2% of the time, Pallas kernels for 0%

profile of v1, /device:TPU:0, one launch (start us, length us, event | category | flops | bytes accessed | tf_op | source)
XLA Modules:
  0.0 1354.0 jit_solution(14916371349976675883)
XLA Ops:
  19.9 92.5 %all-to-all-done = f32[8,1,131072]{2,1,0:T(1,128)} async-done(((f32[8,1,131072]{2,1,0:T(1,128)}), f32[8,1,131072]{2,1,0:T(1,128)}, u32[]{:S(2)}, u32[]{:S(2)}) %all-to-all-start) | async-done | bytes 4194336 | tf_op jit(solution)/shard_map/all_to_all | solution.py:27
  112.4 60.4 %gather_fusion.3 = f32[5120]{0:T(1024)S(1)} fusion(f32[1048576]{0:T(1024)} %bitcast.3, s32[5120]{0:T(1024)S(1)} %broadcast_clamp_fusion), kind=kCustom, calls=%fused_computation.3 | custom fusion | bytes 61440 | tf_op jit(solution)/shard_map/gather | solution.py:39
  172.8 60.4 %gather_fusion.2 = f32[5120]{0:T(1024)S(1)} fusion(f32[1048576]{0:T(1024)} %bitcast.3, s32[5120]{0:T(1024)S(1)} %broadcast_clamp_fusion.1), kind=kCustom, calls=%fused_computation.2 | custom fusion | bytes 61440 | tf_op jit(solution)/shard_map/gather | solution.py:39
  233.2 60.4 %gather_fusion.1 = f32[5120]{0:T(1024)S(1)} fusion(f32[1048576]{0:T(1024)} %bitcast.3, s32[5120]{0:T(1024)S(1)} %broadcast_clamp_fusion.2), kind=kCustom, calls=%fused_computation.1 | custom fusion | bytes 61440 | tf_op jit(solution)/shard_map/gather | solution.py:39
  293.7 60.4 %gather_fusion = f32[5120]{0:T(1024)S(1)} fusion(f32[1048576]{0:T(1024)} %bitcast.3, s32[5120]{0:T(1024)S(1)} %broadcast_clamp_fusion.3), kind=kCustom, calls=%fused_computation | custom fusion | bytes 61440 | tf_op jit(solution)/shard_map/gather | solution.py:39
  360.1 109.3 %scatter_custom_fusion = f32[1048576]{0:T(1024)} fusion(s32[20480]{0:T(1024)S(1)} %bitcast.85, f32[20480]{0:T(1024)S(1)} %pad_maximum_fusion, f32[]{:T(128)} %constant.207.clone.1), kind=kCustom, calls=%fused_computation.6 | custom fusion | flops 20480 | bytes 4194308 | tf_op jit(solution)/shard_map/scatter-add | solution.py:46
  490.7 134.4 %all-reduce.4.cloned.1.call-done = f32[1048576]{0:T(1024)} async-done(((f32[1048576]{0:T(1024)}), f32[1048576]{0:T(1024)}) %all-reduce.4.cloned.1.call-update) | async-done | bytes 4194320 | tf_op jit(solution)/shard_map/psum | solution.py:47
  626.9 16.6 %fusion.61 = (f32[1,131072]{1,0:T(1,128)}, f32[1,131072]{1,0:T(1,128)S(1)}, f32[1,131072]{1,0:T(1,128)}, f32[1,131072]{1,0:T(1,128)S(1)}, f32[1,131072]{1,0:T(1,...) fusion(f32[8,131072]{1,0:T(8,128)} %param.11), kind=kLoop, calls=%fused_computation.206 | loop fusion | bytes 8388608 | tf_op jit(solution)/shard_map/slice | solution.py:66
  643.5 39.4 %all-reduce.1 = (f32[8]{0:T(128)S(1)}, f32[]{:T(128)}) all-reduce(f32[8]{0:T(128)S(1)} %multiply_reduce_fusion, f32[]{:T(128)} %multiply_reduce_fusion.16), channel_id=1, replica_groups=mesh['dp'=8,'table'=4] {'dp','table'}, use_global_device_ids=true, to_apply=%region_1.2 | all-reduce | flops 9 | bytes 72 | tf_op jit(solution)/shard_map/psum | solution.py:52
  687.9 40.3 %psum.145 = f32[]{:T(128)} all-reduce(f32[]{:T(128)} %get-tuple-element.23), channel_id=1, replica_groups=mesh['dp'=8,'table'=4] {'dp','table'}, use_global_device_ids=true, to_apply=%region_14.15 | all-reduce | flops 1 | bytes 8 | tf_op jit(solution)/shard_map/psum | solution.py:63
  731.3 40.5 %psum.146 = f32[]{:T(128)} all-reduce(f32[]{:T(128)} %multiply_reduce_fusion.14), channel_id=1, replica_groups=mesh['dp'=8,'table'=4] {'dp','table'}, use_global_device_ids=true, to_apply=%region_16.17 | all-reduce | flops 1 | bytes 8 | tf_op jit(solution)/shard_map/psum | solution.py:63
  776.0 40.4 %psum.147 = f32[]{:T(128)} all-reduce(f32[]{:T(128)} %get-tuple-element.21), channel_id=1, replica_groups=mesh['dp'=8,'table'=4] {'dp','table'}, use_global_device_ids=true, to_apply=%region_18.19 | all-reduce | flops 1 | bytes 8 | tf_op jit(solution)/shard_map/psum | solution.py:63
  819.6 40.6 %psum.148 = f32[]{:T(128)} all-reduce(f32[]{:T(128)} %multiply_reduce_fusion.12), channel_id=1, replica_groups=mesh['dp'=8,'table'=4] {'dp','table'}, use_global_device_ids=true, to_apply=%region_20.21 | all-reduce | flops 1 | bytes 8 | tf_op jit(solution)/shard_map/psum | solution.py:63
  864.5 40.3 %psum.149 = f32[]{:T(128)} all-reduce(f32[]{:T(128)} %get-tuple-element.19), channel_id=1, replica_groups=mesh['dp'=8,'table'=4] {'dp','table'}, use_global_device_ids=true, to_apply=%region_22.23 | all-reduce | flops 1 | bytes 8 | tf_op jit(solution)/shard_map/psum | solution.py:63
  908.6 40.6 %psum.150 = f32[]{:T(128)} all-reduce(f32[]{:T(128)} %multiply_reduce_fusion.10), channel_id=1, replica_groups=mesh['dp'=8,'table'=4] {'dp','table'}, use_global_device_ids=true, to_apply=%region_24.25 | all-reduce | flops 1 | bytes 8 | tf_op jit(solution)/shard_map/psum | solution.py:63
  953.3 40.4 %all-reduce = (f32[]{:T(128)}, f32[]{:T(128)}) all-reduce(f32[]{:T(128)} %get-tuple-element.17, f32[]{:T(128)} %get-tuple-element.61), channel_id=1, replica_groups=mesh['dp'=8,'table'=4] {'dp','table'}, use_global_device_ids=true, to_apply=%region_26.27 | all-reduce | flops 2 | bytes 16 | tf_op jit(solution)/shard_map/psum | solution.py:63
  998.3 40.6 %psum.152 = f32[]{:T(128)} all-reduce(f32[]{:T(128)} %multiply_reduce_fusion.8), channel_id=1, replica_groups=mesh['dp'=8,'table'=4] {'dp','table'}, use_global_device_ids=true, to_apply=%region_28.29 | all-reduce | flops 1 | bytes 8 | tf_op jit(solution)/shard_map/psum | solution.py:69
  1043.2 40.1 %psum.153 = f32[]{:T(128)} all-reduce(f32[]{:T(128)} %get-tuple-element.15), channel_id=1, replica_groups=mesh['dp'=8,'table'=4] {'dp','table'}, use_global_device_ids=true, to_apply=%region_30.31 | all-reduce | flops 1 | bytes 8 | tf_op jit(solution)/shard_map/psum | solution.py:69
  1086.4 40.7 %psum.154 = f32[]{:T(128)} all-reduce(f32[]{:T(128)} %multiply_reduce_fusion.6), channel_id=1, replica_groups=mesh['dp'=8,'table'=4] {'dp','table'}, use_global_device_ids=true, to_apply=%region_32.33 | all-reduce | flops 1 | bytes 8 | tf_op jit(solution)/shard_map/psum | solution.py:69
  1131.3 40.1 %psum.155 = f32[]{:T(128)} all-reduce(f32[]{:T(128)} %get-tuple-element.13), channel_id=1, replica_groups=mesh['dp'=8,'table'=4] {'dp','table'}, use_global_device_ids=true, to_apply=%region_34.35 | all-reduce | flops 1 | bytes 8 | tf_op jit(solution)/shard_map/psum | solution.py:69
  1174.8 40.7 %psum.156 = f32[]{:T(128)} all-reduce(f32[]{:T(128)} %multiply_reduce_fusion.4), channel_id=1, replica_groups=mesh['dp'=8,'table'=4] {'dp','table'}, use_global_device_ids=true, to_apply=%region_36.37 | all-reduce | flops 1 | bytes 8 | tf_op jit(solution)/shard_map/psum | solution.py:69
  1219.0 40.2 %psum.157 = f32[]{:T(128)} all-reduce(f32[]{:T(128)} %get-tuple-element.11), channel_id=1, replica_groups=mesh['dp'=8,'table'=4] {'dp','table'}, use_global_device_ids=true, to_apply=%region_38.39 | all-reduce | flops 1 | bytes 8 | tf_op jit(solution)/shard_map/psum | solution.py:69
  1261.3 40.6 %psum.158 = f32[]{:T(128)} all-reduce(f32[]{:T(128)} %multiply_reduce_fusion.2), channel_id=1, replica_groups=mesh['dp'=8,'table'=4] {'dp','table'}, use_global_device_ids=true, to_apply=%region_40.41 | all-reduce | flops 1 | bytes 8 | tf_op jit(solution)/shard_map/psum | solution.py:69
  1304.9 40.2 %psum.159 = f32[]{:T(128)} all-reduce(f32[]{:T(128)} %get-tuple-element.9), channel_id=1, replica_groups=mesh['dp'=8,'table'=4] {'dp','table'}, use_global_device_ids=true, to_apply=%region_42.43 | all-reduce | flops 1 | bytes 8 | tf_op jit(solution)/shard_map/psum | solution.py:69
  (77 shorter events, 78.2 us)
Async XLA Ops:
  11.7 7.5 copy-start.4
  11.7 7.5 copy-start.5
  11.7 100.7 %all-to-all-start = ((f32[8,1,131072]{2,1,0:T(1,128)}), f32[8,1,131072]{2,1,0:T(1,128)}, u32[]{:S(2)}, u32[]{:S(2)}) async-start(f32[8,1,131072]{2,1,0:T(1,128)} %stack.2), calls=%async_computation | async-start | bytes 8388608 | tf_op jit(solution)/shard_map/all_to_all | solution.py:27
  19.1 606.1 %all-reduce.4.cloned.1.call-start = ((), (), s32[]{:S(2)}) async-start(), calls=%async_computation.1 | async-start | bytes 8388608 | tf_op jit(solution)/shard_map/psum | solution.py:47
  293.6 66.3 %copy-start.6 = (s32[256]{0:T(256)S(1)}, s32[256]{0:T(256)}, u32[]{:S(2)}) copy-start(s32[256]{0:T(256)} %param.8) | copy-start | bytes 3076
  485.8 139.4 %copy-start = (f32[1,131072]{1,0:T(1,128)}, f32[1,131072]{1,0:T(1,128)S(1)}, u32[]{:S(2)}) copy-start(f32[1,131072]{1,0:T(1,128)S(1)} %get-tuple-element.59) | copy-start | bytes 1572868
  485.8 139.4 %copy-start.2 = (f32[131072]{0:T(1024)S(1)}, f32[131072]{0:T(1024)}, u32[]{:S(2)}) copy-start(f32[131072]{0:T(1024)} %param.9) | copy-start | bytes 1572868
  1128.4 174.7 %copy-start.3 = (f32[1,131072]{1,0:T(1,128)S(1)}, f32[1,131072]{1,0:T(1,128)}, u32[]{:S(2)}) copy-start(f32[1,131072]{1,0:T(1,128)} %get-tuple-element.58) | copy-start | bytes 1572868
  1172.8 173.5 %copy-start.1 = (f32[1,131072]{1,0:T(1,128)S(1)}, f32[1,131072]{1,0:T(1,128)}, u32[]{:S(2)}) copy-start(f32[1,131072]{1,0:T(1,128)} %copy-done) | copy-start | bytes 1572868
Sparse Core Ops, SparseCore 0:
  469.5 155.6 all-reduce.3
